TPU v7x, 512 devices: a whole 4x8x8 slice. The times are simulated.
512 devices in a mesh: blk: 64 (over x, y, core), spec: 8 (over z).
Axes of the slice: x: 4, y: 8, z: 8, core: 2. Of those that a mesh axis runs over, the one named last changes fastest.
Arguments:
- spectrum: float32 [32, 24, 65536], P('spec', None, 'blk'), may hold values from 0.05 to 2
- depths: float32 [65536], P('blk'), may hold values from 5 to 4000
- currents: float32 [2, 65536], P(None, 'blk'), may hold values from -4 to 4
- slopes: float32 [2, 65536], P(None, 'blk'), may hold values from -0.12 to 0.12
- wind_speed: float32 [2, 65536], P(None, 'blk'), may hold values from -40 to 40
- wet_mask: int32 [65536], P('blk'), may hold values 0 or 1
- face_owner: int32 [4096, 1], P('blk'), may hold values from 0 to 63, as said below
- face_block: int32 [4096], P('blk'), may hold values from 0 to 15
- freq_weights: bfloat16 [2, 32, 32], replicated, may hold values from 0.0049743652 to 0.079589844
- angle_weights: bfloat16 [2, 2, 24, 24], replicated, may hold values from 0.0049743652 to 0.099609375
- transfer_rate: float32 [32], replicated, may hold values from 0.05 to 0.3
Outputs:
- next_spectrum: float32 [32, 24, 65536], P('spec', None, 'blk')
Inputs may be any that keep to these rules, and one draw needn't show every extreme that they name: `face_owner`: face i of one device is side i % 4 (west, east, south, north) of its block i // 4. Of the 64 rows of one device, 32 name another index and the rest name the device itself; no other index is named more than 2 times in those rows, and one is named exactly 2 times.
All inputs are finite; a program needn't handle non-finite values. No bound on the sum of `wet_mask` on one device may be relied on, other than what follows from the above.
Results may differ from a plain program's by a relative error of at most 0.0011.
The roundings to bfloat16 on the way count: a program that leaves them out, or rounds other values in their place, can miss the bound.
Values may be sent and summed in bfloat16 or wider, within the bound.
A program may use at most 64 MiB of HBM per device.

v0:
```python
import math
import jax
import jax.numpy as jnp
from jax import lax
from jax.sharding import PartitionSpec as P

TILE = 8
GRAVITY = 9.81
TIME_STEP = 200.0
CELL_SIZE = 5500.0
LOWEST_FREQ = 0.0418
FREQ_GROWTH = 1.1
WIND_GROWTH = 0.0003
TURN_LIMIT = 0.9


def dispersion(radian_freq, water_depth):
    deep_kh = radian_freq * radian_freq / GRAVITY * water_depth
    wave_kh = deep_kh / jnp.sqrt(jnp.tanh(deep_kh))
    decay_two = jnp.exp(-2.0 * wave_kh)
    denom_term = 1.0 - decay_two * decay_two
    shoal_ratio = 4.0 * wave_kh * decay_two / denom_term
    phase_speed = radian_freq * water_depth / wave_kh
    group_speed = 0.5 * (1.0 + shoal_ratio) * phase_speed
    turn_factor = 2.0 * radian_freq * decay_two / denom_term
    return (phase_speed, group_speed, turn_factor)


def courants(radian_freq, angle_values, water_depth, current_xy, slope_xy, wet_float):
    freq_column = radian_freq[:, None, None, None, None]
    phase_speed, group_speed, turn_factor = dispersion(freq_column, water_depth[None, None])
    cosine = jnp.cos(angle_values)[None, :, None, None, None]
    sine = jnp.sin(angle_values)[None, :, None, None, None]
    grid_ratio = TIME_STEP / CELL_SIZE
    cour_x = (group_speed * cosine + current_xy[0][None, None]) * grid_ratio * wet_float[None, None]
    cour_y = (group_speed * sine + current_xy[1][None, None]) * grid_ratio * wet_float[None, None]
    angle_step = 2.0 * math.pi / angle_values.shape[0]
    turning = (
        turn_factor
        * (sine * slope_xy[0][None, None] - cosine * slope_xy[1][None, None])
        * (TIME_STEP / angle_step)
    )
    cour_turn = jnp.clip(turning, -TURN_LIMIT, TURN_LIMIT)
    return (phase_speed, cour_x, cour_y, cour_turn)


def edge_fluxes(wave_field, cour_x, cour_y):
    west_side = jnp.maximum(-cour_x[..., :, 0], 0.0) * wave_field[..., :, 0]
    east_side = jnp.maximum(cour_x[..., :, -1], 0.0) * wave_field[..., :, -1]
    south_side = jnp.maximum(-cour_y[..., 0, :], 0.0) * wave_field[..., 0, :]
    north_side = jnp.maximum(cour_y[..., -1, :], 0.0) * wave_field[..., -1, :]
    return jnp.stack([west_side, east_side, south_side, north_side], axis=3)


def transported(wave_field, cour_x, cour_y, cour_turn, inflow):
    tile_side = wave_field.shape[-1]
    rightward = jnp.maximum(cour_x, 0.0) * wave_field
    leftward = jnp.maximum(-cour_x, 0.0) * wave_field
    upward = jnp.maximum(cour_y, 0.0) * wave_field
    downward = jnp.maximum(-cour_y, 0.0) * wave_field
    lead_pads = [(0, 0)] * 3
    from_x = jnp.pad(rightward[..., :, :-1], lead_pads + [(0, 0), (1, 0)]) + jnp.pad(
        leftward[..., :, 1:], lead_pads + [(0, 0), (0, 1)]
    )
    from_y = jnp.pad(upward[..., :-1, :], lead_pads + [(1, 0), (0, 0)]) + jnp.pad(
        downward[..., 1:, :], lead_pads + [(0, 1), (0, 0)]
    )
    from_turn = jnp.roll(jnp.maximum(cour_turn, 0.0) * wave_field, 1, axis=1) + jnp.roll(
        jnp.maximum(-cour_turn, 0.0) * wave_field, -1, axis=1
    )
    ghost_x = jnp.pad(inflow[:, :, :, 0, :, None], lead_pads + [(0, 0), (0, tile_side - 1)])
    ghost_x = ghost_x + jnp.pad(
        inflow[:, :, :, 1, :, None], lead_pads + [(0, 0), (tile_side - 1, 0)]
    )
    ghost_y = jnp.pad(inflow[:, :, :, 2, None, :], lead_pads + [(0, tile_side - 1), (0, 0)])
    ghost_y = ghost_y + jnp.pad(
        inflow[:, :, :, 3, None, :], lead_pads + [(tile_side - 1, 0), (0, 0)]
    )
    outflow = (jnp.abs(cour_x) + jnp.abs(cour_y) + jnp.abs(cour_turn)) * wave_field
    return wave_field - outflow + from_x + from_y + from_turn + ghost_x + ghost_y


def nonlinear(levels, freq_weights, angle_weights, transfer_rate):
    levels_wide = levels.astype(jnp.float32)
    shifted_plus = jnp.einsum(
        "gf,fdq->gdq", freq_weights[0], levels, preferred_element_type=jnp.float32
    ).astype(jnp.bfloat16)
    shifted_minus = jnp.einsum(
        "gf,fdq->gdq", freq_weights[1], levels, preferred_element_type=jnp.float32
    ).astype(jnp.bfloat16)
    rate_column = transfer_rate[:, None, None]
    delta_list = []
    for mirror in range(2):
        image_plus = jnp.einsum(
            "ed,gdq->geq",
            angle_weights[mirror, 0],
            shifted_plus,
            preferred_element_type=jnp.float32,
        )
        image_minus = jnp.einsum(
            "ed,gdq->geq",
            angle_weights[mirror, 1],
            shifted_minus,
            preferred_element_type=jnp.float32,
        )
        delta_list.append(
            rate_column
            * (
                levels_wide * levels_wide * (image_plus + image_minus)
                - 2.0 * levels_wide * image_plus * image_minus
            )
        )
    low_first = delta_list[0].astype(jnp.bfloat16)
    low_second = delta_list[1].astype(jnp.bfloat16)
    back_plus = (
        jnp.einsum(
            "ed,geq->gdq", angle_weights[0, 0], low_first, preferred_element_type=jnp.float32
        )
        + jnp.einsum(
            "ed,geq->gdq", angle_weights[1, 0], low_second, preferred_element_type=jnp.float32
        )
    ).astype(jnp.bfloat16)
    back_minus = (
        jnp.einsum(
            "ed,geq->gdq", angle_weights[0, 1], low_first, preferred_element_type=jnp.float32
        )
        + jnp.einsum(
            "ed,geq->gdq", angle_weights[1, 1], low_second, preferred_element_type=jnp.float32
        )
    ).astype(jnp.bfloat16)
    spread_plus = jnp.einsum(
        "gf,gdq->fdq", freq_weights[0], back_plus, preferred_element_type=jnp.float32
    )
    spread_minus = jnp.einsum(
        "gf,gdq->fdq", freq_weights[1], back_minus, preferred_element_type=jnp.float32
    )
    return -2.0 * (delta_list[0] + delta_list[1]) + spread_plus + spread_minus


def shards(
    spectrum,
    depths,
    currents,
    slopes,
    wind_speed,
    wet_mask,
    face_owner,
    face_block,
    freq_weights,
    angle_weights,
    transfer_rate,
):
    freq_local, angle_count, point_count = spectrum.shape
    block_count = point_count // (TILE * TILE)
    group_count = lax.axis_size("spec")
    peer_count = lax.axis_size("blk")
    my_index = lax.axis_index("blk")
    face_count = face_block.shape[0]
    remote_total = face_count // 2
    capacity = max(2, (remote_total + peer_count - 2) // (peer_count - 1))
    first_freq = lax.axis_index("spec") * freq_local
    freq_index = (first_freq + jnp.arange(freq_local, dtype=jnp.int32)).astype(jnp.float32)
    radian_freq = 2.0 * math.pi * LOWEST_FREQ * jnp.power(jnp.float32(FREQ_GROWTH), freq_index)
    angle_values = jnp.arange(angle_count, dtype=jnp.int32).astype(jnp.float32) * (
        2.0 * math.pi / angle_count
    )
    wet_float = wet_mask.astype(jnp.float32)
    wave_field = spectrum.reshape(freq_local, angle_count, block_count, TILE, TILE)
    phase_speed, cour_x, cour_y, cour_turn = courants(
        radian_freq,
        angle_values,
        depths.reshape(block_count, TILE, TILE),
        currents.reshape(2, block_count, TILE, TILE),
        slopes.reshape(2, block_count, TILE, TILE),
        wet_float.reshape(block_count, TILE, TILE),
    )
    edges = edge_fluxes(wave_field, cour_x, cour_y)
    edge_rows = edges.transpose(2, 3, 0, 1, 4).reshape(
        block_count * 4, freq_local * angle_count * TILE
    )
    owners = face_owner[:, 0]
    face_sides = jnp.arange(face_count, dtype=jnp.int32) % 4
    wanted_ids = face_block * 4 + jnp.bitwise_xor(face_sides, 1)
    remote_face = (owners != my_index).astype(jnp.int32)
    peer_onehot = (owners[:, None] == jnp.arange(peer_count, dtype=jnp.int32)[None, :]).astype(
        jnp.int32
    ) * remote_face[:, None]
    earlier = jnp.cumsum(peer_onehot, axis=0) - peer_onehot
    slot_ranks = jnp.sum(earlier * peer_onehot, axis=1)
    slot_range = jnp.arange(capacity, dtype=jnp.int32)
    slot_onehot = (slot_ranks[:, None] == slot_range[None, :]).astype(jnp.int32)
    requests = jnp.sum(
        peer_onehot[:, :, None] * (slot_onehot * wanted_ids[:, None])[:, None, :], axis=0
    )
    located = jnp.take(
        edge_rows, lax.all_to_all(requests, "blk", split_axis=0, concat_axis=0, tiled=True), axis=0
    )
    replies = lax.all_to_all(located, "blk", split_axis=0, concat_axis=0, tiled=True)
    remote_index = jnp.where(remote_face > 0, owners * capacity + slot_ranks, 0)
    remote_rows = jnp.take(replies.reshape(peer_count * capacity, -1), remote_index, axis=0)
    local_rows = jnp.take(edge_rows, wanted_ids, axis=0)
    inflow_rows = jnp.where(remote_face[:, None] > 0, remote_rows, local_rows)
    inflow = inflow_rows.reshape(block_count, 4, freq_local, angle_count, TILE).transpose(
        2, 3, 0, 1, 4
    )
    moved = transported(wave_field, cour_x, cour_y, cour_turn, inflow).reshape(
        freq_local, angle_count, point_count
    )
    levels = moved.astype(jnp.bfloat16).reshape(
        freq_local, angle_count, group_count, point_count // group_count
    )
    result = nonlinear(
        lax.all_to_all(levels, "spec", split_axis=2, concat_axis=0, tiled=True)[:, :, 0, :],
        freq_weights,
        angle_weights,
        transfer_rate,
    )
    item_width = result.shape[2]
    split_rows = result.reshape(group_count, freq_local, angle_count, item_width)
    returned = lax.all_to_all(split_rows, "spec", split_axis=0, concat_axis=0, tiled=True)
    transfer = returned.transpose(1, 2, 0, 3).reshape(freq_local, angle_count, point_count)
    along_wind = (
        wind_speed[0][None, None, :] * jnp.cos(angle_values)[None, :, None]
        + wind_speed[1][None, None, :] * jnp.sin(angle_values)[None, :, None]
    )
    phase_flat = phase_speed.reshape(freq_local, 1, point_count)
    growth = (
        TIME_STEP
        * WIND_GROWTH
        * radian_freq[:, None, None]
        * jnp.maximum(along_wind / phase_flat - 1.0, 0.0)
    )
    return wet_float[None, None, :] * (moved + transfer + growth * moved)


def solution(mesh):
    in_specs = (
        P("spec", None, "blk"),
        P("blk"),
        P(None, "blk"),
        P(None, "blk"),
        P(None, "blk"),
        P("blk"),
        P("blk", None),
        P("blk"),
        P(),
        P(),
        P(),
    )
    out_specs = P("spec", None, "blk")
    return jax.shard_map(shards, mesh=mesh, in_specs=in_specs, out_specs=out_specs, check_vma=False)
```

profile of v0, /device:TPU:6, one launch (start us, length us, event | category | flops | bytes accessed | tf_op | source)
XLA Modules:
  0.0 151.9 jit_solution(5503527234569175041)
XLA Ops:
  4.9 11.0 %all-to-all-start = ((s32[64,1,2]{2,1,0:T(1,128)}), s32[64,1,2]{2,1,0:T(1,128)}, u32[]{:S(2)}, u32[]{:S(2)}) async-start(s32[64,1,2]{2,1,0:T(1,128)} %copy.142), calls=%async_computation | async-start | bytes 65536 | tf_op jit(solution)/shard_map/all_to_all | solution.py:196
  20.3 1.6 %copy.138 = f32[4,24,1024]{1,2,0:T(8,128)S(1)} copy(f32[4,24,1024]{2,1,0:T(8,128)} %param.11) | data formatting | bytes 786432 | tf_op args[0]
  23.0 1.4 copy-done
  30.0 2.4 %maximum_multiply_fusion.1 = (f32[4,24,16,8,8]{1,4,3,2,0:T(8,128)}, f32[4,24,16,8,8]{1,4,3,2,0:T(8,128)}) fusion(f32[4,24,16,8,8]{1,4,3,2,0:T(8,128)S(1)} %bitcast.143, f32[24,16,8,8]{0,3,2,1:T(8,128)S(1)} %multiply_subtract_fusion.1, f32[4,16,8,8]{3,2,1,0:T(8,128)S(1)} %copy.141), kind=kLoop, calls=%fused_computation.17 | loop fusion | flops 786432 | bytes 1294336 | tf_op jit(solution)/shard_map/mul | solution.py:68
  33.6 3.2 %copy.145 = f32[16,4,4,24,8]{4,3,2,1,0:T(8,128)} copy(f32[16,4,4,24,8]{3,4,1,0,2:T(8,128)} %maximum_bitcast_fusion) | data formatting | bytes 393216 | tf_op jit(solution)/shard_map/transpose | solution.py:178
  36.8 3.4 %reshape.422 = f32[64,768]{1,0:T(8,128)S(1)} reshape(f32[16,4,4,24,8]{4,3,2,1,0:T(8,128)} %copy.145) | data formatting | bytes 393216 | tf_op jit(solution)/shard_map/reshape | solution.py:178
  40.9 3.4 %gather.20 = f32[16,4,4,24,8]{4,3,2,1,0:T(8,128)} reshape(f32[64,768]{1,0:T(8,128)S(1)} %gather_fusion.2) | data formatting | bytes 393216 | tf_op jit(solution)/shard_map/jit(_take)/gather | solution.py:201
  44.2 3.2 %copy.149 = f32[16,4,4,24,8]{3,4,1,0,2:T(8,128)} copy(f32[16,4,4,24,8]{4,3,2,1,0:T(8,128)} %gather.20) | data formatting | bytes 393216 | tf_op jit(solution)/shard_map/jit(_take)/gather | solution.py:201
  48.3 3.7 %slice.162 = f32[4,1,16,8,8]{1,4,3,2,0:T(8,128)} slice(f32[4,24,16,8,8]{1,4,3,2,0:T(8,128)} %get-tuple-element.23), slice={[0:4], [23:24], [0:16], [0:8], [0:8]} | slice | bytes 32768 | tf_op jit(solution)/shard_map/jit(_roll_static)/slice | solution.py:68
  51.9 2.0 %slice.164 = f32[4,23,16,8,8]{1,4,3,2,0:T(8,128)} slice(f32[4,24,16,8,8]{1,4,3,2,0:T(8,128)S(1)} %copy-done.3), slice={[0:4], [1:24], [0:16], [0:8], [0:8]} | slice | bytes 753664 | tf_op jit(solution)/shard_map/jit(_roll_static)/slice | solution.py:68
  55.6 1.6 %gather_fusion = f32[128,768]{1,0:T(8,128)} fusion(f32[64,768]{1,0:T(8,128)S(1)} %reshape.422, s32[1024]{0:T(1024)S(1)} %pad_clamp_fusion.2), kind=kCustom, calls=%fused_computation | custom fusion | bytes 786944 | tf_op jit(solution)/shard_map/jit(_take)/gather | solution.py:195
  60.0 10.5 %all-to-all-start.1 = ((f32[64,2,768]{2,1,0:T(2,128)}), f32[64,2,768]{2,1,0:T(2,128)}, u32[]{:S(2)}, u32[]{:S(2)}) async-start(f32[64,2,768]{2,1,0:T(2,128)} %broadcast_select_fusion), calls=%async_computation.1 | async-start | bytes 786432 | tf_op jit(solution)/shard_map/all_to_all | solution.py:198
  70.5 4.4 %slice_multiply_fusion.3 = (f32[4,24,16,7,8]{1,4,3,2,0:T(8,128)}, f32[4,24,16,7,8]{1,4,3,2,0:T(8,128)}) fusion(f32[4,24,16,8,8]{1,4,3,2,0:T(8,128)S(1)} %bitcast.144, f32[4,24,16,8,8]{1,4,3,2,0:T(8,128)} %copy-done.5), kind=kLoop, calls=%fused_computation.24 | loop fusion | flops 430080 | bytes 2064384 | tf_op jit(solution)/shard_map/mul | solution.py:59
  75.0 2.6 %slice_multiply_fusion.1 = (f32[4,24,16,8,7]{1,4,3,2,0:T(8,128)}, f32[4,24,16,8,7]{1,4,3,2,0:T(8,128)}) fusion(f32[4,24,16,8,8]{1,4,3,2,0:T(8,128)S(1)} %bitcast.145, f32[4,24,16,8,8]{1,4,3,2,0:T(8,128)S(1)} %copy-done.1), kind=kLoop, calls=%fused_computation.12 | loop fusion | flops 430080 | bytes 2064384 | tf_op jit(solution)/shard_map/mul | solution.py:57
  77.6 7.0 %all-to-all-done.1 = f32[64,2,768]{2,1,0:T(2,128)} async-done(((f32[64,2,768]{2,1,0:T(2,128)}), f32[64,2,768]{2,1,0:T(2,128)}, u32[]{:S(2)}, u32[]{:S(2)}) %all-to-all-start.1) | async-done | bytes 393248 | tf_op jit(solution)/shard_map/all_to_all | solution.py:198
  85.9 1.5 gather_fusion.1
  87.3 3.8 %gather.18 = f32[16,4,4,24,8]{4,3,2,1,0:T(8,128)} reshape(f32[64,768]{1,0:T(8,128)} %gather_fusion.1) | data formatting | bytes 393216 | tf_op jit(solution)/shard_map/jit(_take)/gather | solution.py:200
  91.2 3.2 %copy.148 = f32[16,4,4,24,8]{3,4,1,0,2:T(8,128)} copy(f32[16,4,4,24,8]{4,3,2,1,0:T(8,128)} %gather.18) | data formatting | bytes 393216 | tf_op jit(solution)/shard_map/jit(_take)/gather | solution.py:200
  94.3 2.0 %select_bitcast_fusion = f32[4,24,16,4,8]{1,4,3,2,0:T(8,128)S(1)} fusion(f32[16,4,4,24,8]{3,4,1,0,2:T(8,128)} %copy.149, f32[16,4,4,24,8]{3,4,1,0,2:T(8,128)} %copy.148, pred[16,4]{1,0:T(8,128)(4,1)S(1)} %copy-done.28, pred[16,4]{1,0:T(8,128)(4,1)S(1)} %broadcast_in_dim.64, pred[16,4]{1,0:T(8,128)(4,1)S(1)} %broadcast_in_dim.62), kind=kLoop, calls=%fused_computation.41 | loop fusion | flops 147456 | bytes 590016 | tf_op jit(solution)/shard_map/transpose | solution.py:203
  98.7 7.7 %fusion.97 = (bf16[4,24,16,8,8]{1,4,3,2,0:T(8,128)(2,1)}, f32[4,24,16,8,8]{1,4,3,2,0:T(8,128)}) fusion(f32[4,24,16,1,8]{1,4,3,2,0:T(8,128)S(1)} %get-tuple-element.26, f32[4,24,16,1,8]{1,4,3,2,0:T(8,128)S(1)} %get-tuple-element.27, f32[4,24,16,8,8]{1,3,2,0,4:T(8,128)S(1)} %pad_add_fusion, f32[4,1,16,8,8]{1,4,3,2,0:T(8,128)S(1)} %bitcast.148, ...), kind=kLoop, calls=%fused_computation.176 | loop fusion | flops 2752512 | bytes 3780800 | tf_op jit(solution)/shard_map/convert_element_type | solution.py:209
  106.3 1.6 %copy.152 = bf16[4,24,8,128]{3,1,0,2:T(8,128)(2,1)S(1)} copy(bf16[4,24,8,128]{1,3,2,0:T(8,128)(2,1)} %bitcast.154) | data formatting | bytes 393216 | tf_op jit(solution)/shard_map/convert_element_type | solution.py:209
  107.9 21.1 %all_to_all.40 = bf16[4,24,8,128]{3,1,0,2:T(8,128)(2,1)S(1)} all-to-all(bf16[4,24,8,128]{3,1,0,2:T(8,128)(2,1)S(1)} %copy.152), channel_id=1, replica_groups=mesh['blk'=64,'spec'=8] {'spec'}, dimensions={2} | all-to-all | bytes 393216 | tf_op jit(solution)/shard_map/all_to_all | solution.py:213
  133.3 3.5 %all-to-all-start.3 = ((f32[8,4,24,128]{3,1,2,0:T(4,128)}), f32[8,4,24,128]{3,1,2,0:T(4,128)S(1)}, u32[]{:S(2)}, u32[]{:S(2)}) async-start(f32[8,4,24,128]{3,1,2,0:T(4,128)} %copy.174), calls=%async_computation.3 | async-start | bytes 786432 | tf_op jit(solution)/shard_map/all_to_all | solution.py:220
  137.6 13.1 %all-to-all-done.3 = f32[8,4,24,128]{3,1,2,0:T(4,128)S(1)} async-done(((f32[8,4,24,128]{3,1,2,0:T(4,128)}), f32[8,4,24,128]{3,1,2,0:T(4,128)S(1)}, u32[]{:S(2)}, u32[]{:S(2)}) %all-to-all-start.3) | async-done | bytes 393248 | tf_op jit(solution)/shard_map/all_to_all | solution.py:220
  (146 shorter events, 32.4 us)
Async XLA Ops:
  4.9 49.0 %all-to-all-start = ((s32[64,1,2]{2,1,0:T(1,128)}), s32[64,1,2]{2,1,0:T(1,128)}, u32[]{:S(2)}, u32[]{:S(2)}) async-start(s32[64,1,2]{2,1,0:T(1,128)} %copy.142), calls=%async_computation | async-start | bytes 65536 | tf_op jit(solution)/shard_map/all_to_all | solution.py:196
  15.9 7.0 %copy-start.29 = (f32[4]{0:T(128)}, f32[4]{0:T(128)S(1)}, u32[]{:S(2)}) copy-start(f32[4]{0:T(128)S(1)} %get-tuple-element.41) | copy-start | bytes 52
  16.0 7.0 %copy-start.31 = (f32[4]{0:T(128)}, f32[4]{0:T(128)S(1)}, u32[]{:S(2)}) copy-start(f32[4]{0:T(128)S(1)} %broadcast_multiply_fusion.3) | copy-start | bytes 52
  16.0 12.7 %copy-start.21 = (f32[24]{0:T(128)}, f32[24]{0:T(128)S(1)}, u32[]{:S(2)}) copy-start(f32[24]{0:T(128)S(1)} %get-tuple-element.43) | copy-start | bytes 292
  16.0 12.7 %copy-start.24 = (f32[24]{0:T(128)}, f32[24]{0:T(128)S(1)}, u32[]{:S(2)}) copy-start(f32[24]{0:T(128)S(1)} %get-tuple-element.44) | copy-start | bytes 292
  19.3 3.6 %copy-start.11 = (f32[16,8,8]{2,1,0:T(8,128)}, f32[16,8,8]{2,1,0:T(8,128)S(1)}, u32[]{:S(2)}) copy-start(f32[16,8,8]{2,1,0:T(8,128)S(1)} %add.194) | copy-start | bytes 12292
  19.4 3.5 %copy-start.13 = (f32[16,8,8]{2,1,0:T(8,128)}, f32[16,8,8]{2,1,0:T(8,128)S(1)}, u32[]{:S(2)}) copy-start(f32[16,8,8]{2,1,0:T(8,128)S(1)} %add.197) | copy-start | bytes 12292
  44.2 3.3 %copy-start.33 = (pred[64]{0:T(512)(128)(4,1)S(1)}, pred[64]{0:T(512)(128)(4,1)}, u32[]{:S(2)}) copy-start(pred[64]{0:T(512)(128)(4,1)} %get-tuple-element.37) | copy-start | bytes 196
  44.2 3.4 %copy-start.35 = (pred[64]{0:T(512)(128)(4,1)S(1)}, pred[64]{0:T(512)(128)(4,1)}, u32[]{:S(2)}) copy-start(pred[64]{0:T(512)(128)(4,1)} %get-tuple-element.13) | copy-start | bytes 196
  48.3 3.7 %copy-start.3 = (f32[4,24,16,8,8]{1,4,3,2,0:T(8,128)S(1)}, f32[4,24,16,8,8]{1,4,3,2,0:T(8,128)}, u32[]{:S(2)}) copy-start(f32[4,24,16,8,8]{1,4,3,2,0:T(8,128)} %get-tuple-element.24) | copy-start | bytes 1179652
  60.0 24.6 %all-to-all-start.1 = ((f32[64,2,768]{2,1,0:T(2,128)}), f32[64,2,768]{2,1,0:T(2,128)}, u32[]{:S(2)}, u32[]{:S(2)}) async-start(f32[64,2,768]{2,1,0:T(2,128)} %broadcast_select_fusion), calls=%async_computation.1 | async-start | bytes 786432 | tf_op jit(solution)/shard_map/all_to_all | solution.py:198
  70.5 4.4 %copy-start.1 = (f32[4,24,16,8,8]{1,4,3,2,0:T(8,128)S(1)}, f32[4,24,16,8,8]{1,4,3,2,0:T(8,128)}, u32[]{:S(2)}) copy-start(f32[4,24,16,8,8]{1,4,3,2,0:T(8,128)} %copy-done) | copy-start | bytes 1179652
  98.6 30.5 %copy-start.18 = (bf16[2,32,32]{2,1,0:T(8,128)(2,1)S(1)}, bf16[2,32,32]{2,1,0:T(8,128)(2,1)}, u32[]{:S(2)}) copy-start(bf16[2,32,32]{2,1,0:T(8,128)(2,1)} %param.19) | copy-start | bytes 12292
  106.3 23.0 %copy-start.17 = (bf16[2,2,24,24]{3,2,1,0:T(8,128)(2,1)S(1)}, bf16[2,2,24,24]{3,2,1,0:T(8,128)(2,1)}, u32[]{:S(2)}) copy-start(bf16[2,2,24,24]{3,2,1,0:T(8,128)(2,1)} %param.20) | copy-start | bytes 13828
  107.9 22.4 %copy-start.34 = (f32[32]{0:T(128)S(1)}, f32[32]{0:T(128)}, u32[]{:S(2)}) copy-start(f32[32]{0:T(128)} %param.21) | copy-start | bytes 388
  131.7 5.1 %copy-start.19 = (s32[1024]{0:T(1024)S(1)}, s32[1024]{0:T(1024)}, u32[]{:S(2)}) copy-start(s32[1024]{0:T(1024)} %param.16) | copy-start | bytes 12292
  131.7 5.1 %copy-start.27 = (f32[2,1024]{1,0:T(2,128)S(1)}, f32[2,1024]{1,0:T(2,128)}, u32[]{:S(2)}) copy-start(f32[2,1024]{1,0:T(2,128)} %param.15) | copy-start | bytes 24580
  131.7 5.1 %copy-start.20 = (f32[1024]{0:T(1024)S(1)}, f32[1024]{0:T(1024)}, u32[]{:S(2)}) copy-start(f32[1024]{0:T(1024)} %param.12) | copy-start | bytes 12292
  131.7 5.1 %copy-start.30 = (f32[4]{0:T(128)S(1)}, f32[4]{0:T(128)}, u32[]{:S(2)}) copy-start(f32[4]{0:T(128)} %copy-done.29) | copy-start | bytes 52
  131.7 5.1 %copy-start.32 = (f32[4]{0:T(128)S(1)}, f32[4]{0:T(128)}, u32[]{:S(2)}) copy-start(f32[4]{0:T(128)} %copy-done.31) | copy-start | bytes 52
  131.7 5.2 %copy-start.23 = (f32[24]{0:T(128)S(1)}, f32[24]{0:T(128)}, u32[]{:S(2)}) copy-start(f32[24]{0:T(128)} %copy-done.21) | copy-start | bytes 292
  131.7 5.2 %copy-start.26 = (f32[24]{0:T(128)S(1)}, f32[24]{0:T(128)}, u32[]{:S(2)}) copy-start(f32[24]{0:T(128)} %copy-done.24) | copy-start | bytes 292
  131.8 5.3 %copy-start.7 = (f32[4,24,16,8,8]{1,4,3,2,0:T(8,128)S(1)}, f32[4,24,16,8,8]{1,4,3,2,0:T(8,128)}, u32[]{:S(2)}) copy-start(f32[4,24,16,8,8]{1,4,3,2,0:T(8,128)} %get-tuple-element.10) | copy-start | bytes 1179652
  133.3 17.5 %all-to-all-start.3 = ((f32[8,4,24,128]{3,1,2,0:T(4,128)}), f32[8,4,24,128]{3,1,2,0:T(4,128)S(1)}, u32[]{:S(2)}, u32[]{:S(2)}) async-start(f32[8,4,24,128]{3,1,2,0:T(4,128)} %copy.174), calls=%async_computation.3 | async-start | bytes 786432 | tf_op jit(solution)/shard_map/all_to_all | solution.py:220
  (16 other events, 36.0 us)
where the time goes:
time: 153 us; the launch traced here: 152 us
  local copies, waits for them, and re-layouts  47.4 us (31%)
  other arithmetic  34.7 us (23%)
  starting transfers between devices  24.9 us (16%)
  blocking collectives  21.1 us (14%)
  waiting for transfers between devices  20.1 us (13%)
  matrix products  2.79 us (2%)
    all_to_all x1, blocking collectives, shards(): lax.all_to_all(levels, 'spec', split_axis=2, concat_axis=0, tiled=True)  21.1 us
    all_to_all x1, waiting for transfers between devices, shards(): lax.all_to_all(split_rows, 'spec', split_axis=0, concat_axis=0, tiled=True)  13.1 us
    all_to_all x1, starting transfers between devices, shards(): lax.all_to_all(requests, 'blk', split_axis=0, concat_axis=0, tiled=True)  11 us
    all_to_all x1, starting transfers between devices, shards(): lax.all_to_all(located, 'blk', split_axis=0, concat_axis=0, tiled=True)  10.5 us
    gather x3, local copies, waits for them, and re-layouts, shards(): jnp.take(replies.reshape(peer_count * capacity, -1), remote_index, axis=0)  8.47 us
    convert_element_type x1, other arithmetic, shards(): moved.astype(jnp.bfloat16)  7.67 us
    gather x3, local copies, waits for them, and re-layouts, shards(): local_rows = jnp.take(edge_rows, wanted_ids, axis=0)  7.21 us
    all_to_all x1, waiting for transfers between devices, shards(): lax.all_to_all(located, 'blk', split_axis=0, concat_axis=0, tiled=True)  7 us
  transfers between devices with their start and end apart: 3, of which 2 were waited for; matrix products, arithmetic and copies ran while one was open for 29% of the time, Pallas kernels for 0%

commit v1 on v0

--- a/solution.py
+++ b/solution.py
@@ -12,6 +12,12 @@
 FREQ_GROWTH = 1.1
 WIND_GROWTH = 0.0003
 TURN_LIMIT = 0.9
+
+
+def swap_blocks(x, axis, split, join):
+    pieces = jnp.split(x, lax.axis_size(axis), axis=split)
+    incoming = lax.all_to_all(jnp.stack(pieces), axis, 0, 0)
+    return jnp.concatenate(incoming, axis=join)
 
 
 def dispersion(radian_freq, water_depth):
@@ -210,10 +216,7 @@
         freq_local, angle_count, group_count, point_count // group_count
     )
     result = nonlinear(
-        lax.all_to_all(levels, "spec", split_axis=2, concat_axis=0, tiled=True)[:, :, 0, :],
-        freq_weights,
-        angle_weights,
-        transfer_rate,
+        swap_blocks(levels, "spec", 2, 0)[:, :, 0, :], freq_weights, angle_weights, transfer_rate
     )
     item_width = result.shape[2]
     split_rows = result.reshape(group_count, freq_local, angle_count, item_width)

time: 153 us -> 146 us (0.954)
  waiting for transfers between devices: 20.1 us -> 12.7 us
    all_to_all x1, waiting for transfers between devices: 7 us -> 0.01 us  [shards(): lax.all_to_all(located, 'blk', split_axis=0, concat_axis=0, tiled=True)]
    convert_element_type x1 -> x0, local copies, waits for them, and re-layouts: 1.56 us -> none  [shards(): moved.astype(jnp.bfloat16)]
    unnamed x75 -> x70, local copies, waits for them, and re-layouts: 5.03 us -> 5 us
  transfers between devices with their start and end apart: 3 -> 3, of which waited for: 2 -> 1; matrix products, arithmetic and copies ran while one was open for 29% -> 31% of each run, Pallas kernels for 0% -> 0%
where the time goes in v1:
time: 146 us; the launch traced here: 145 us
  local copies, waits for them, and re-layouts  46.9 us (32%)
  other arithmetic  35.8 us (25%)
  starting transfers between devices  24.9 us (17%)
  blocking collectives  20.9 us (14%)
  waiting for transfers between devices  12.7 us (9%)
  matrix products  2.79 us (2%)
    all_to_all x1, blocking collectives, swap_blocks(): incoming = lax.all_to_all(jnp.stack(pieces), axis, 0, 0)  20.9 us
    all_to_all x1, waiting for transfers between devices, shards(): lax.all_to_all(split_rows, 'spec', split_axis=0, concat_axis=0, tiled=True)  12.7 us
    all_to_all x1, starting transfers between devices, shards(): lax.all_to_all(requests, 'blk', split_axis=0, concat_axis=0, tiled=True)  11 us
    all_to_all x1, starting transfers between devices, shards(): lax.all_to_all(located, 'blk', split_axis=0, concat_axis=0, tiled=True)  10.5 us
    gather x3, local copies, waits for them, and re-layouts, shards(): jnp.take(replies.reshape(peer_count * capacity, -1), remote_index, axis=0)  8.47 us
    convert_element_type x1, other arithmetic, shards(): moved.astype(jnp.bfloat16)  7.45 us
    gather x3, local copies, waits for them, and re-layouts, shards(): local_rows = jnp.take(edge_rows, wanted_ids, axis=0)  7.34 us
    unnamed x70, local copies, waits for them, and re-layouts  5 us
  transfers between devices with their start and end apart: 3, of which 1 were waited for; matrix products, arithmetic and copies ran while one was open for 31% of the time, Pallas kernels for 0%

profile of v1, /device:TPU:6, one launch (start us, length us, event | category | flops | bytes accessed | tf_op | source)
XLA Modules:
  0.0 144.9 jit_solution(4871420596746427262)
XLA Ops:
  5.0 11.0 %all-to-all-start = ((s32[64,1,2]{2,1,0:T(1,128)}), s32[64,1,2]{2,1,0:T(1,128)}, u32[]{:S(2)}, u32[]{:S(2)}) async-start(s32[64,1,2]{2,1,0:T(1,128)} %copy.170), calls=%async_computation | async-start | bytes 65536 | tf_op jit(solution)/shard_map/all_to_all | solution.py:202
  20.4 1.6 %copy.166 = f32[4,24,1024]{1,2,0:T(8,128)S(1)} copy(f32[4,24,1024]{2,1,0:T(8,128)} %param.11) | data formatting | bytes 786432 | tf_op args[0]
  24.4 1.3 slice_multiply_fusion.7
  29.4 2.4 %maximum_multiply_fusion.1 = (f32[4,24,16,8,8]{1,4,3,2,0:T(8,128)}, f32[4,24,16,8,8]{1,4,3,2,0:T(8,128)}) fusion(f32[4,24,16,8,8]{1,4,3,2,0:T(8,128)S(1)} %bitcast.156, f32[24,16,8,8]{0,3,2,1:T(8,128)S(1)} %multiply_subtract_fusion.1, f32[4,16,8,8]{3,2,1,0:T(8,128)S(1)} %copy.169), kind=kLoop, calls=%fused_computation.17 | loop fusion | flops 786432 | bytes 1294336 | tf_op jit(solution)/shard_map/mul | solution.py:74
  33.6 3.2 %copy.173 = f32[16,4,4,24,8]{4,3,2,1,0:T(8,128)} copy(f32[16,4,4,24,8]{3,4,1,0,2:T(8,128)} %maximum_bitcast_fusion) | data formatting | bytes 393216 | tf_op jit(solution)/shard_map/transpose | solution.py:184
  36.8 3.4 %reshape.421 = f32[64,768]{1,0:T(8,128)S(1)} reshape(f32[16,4,4,24,8]{4,3,2,1,0:T(8,128)} %copy.173) | data formatting | bytes 393216 | tf_op jit(solution)/shard_map/reshape | solution.py:184
  41.1 3.7 %slice.162 = f32[4,1,16,8,8]{1,4,3,2,0:T(8,128)} slice(f32[4,24,16,8,8]{1,4,3,2,0:T(8,128)} %get-tuple-element.23), slice={[0:4], [23:24], [0:16], [0:8], [0:8]} | slice | bytes 32768 | tf_op jit(solution)/shard_map/jit(_roll_static)/slice | solution.py:74
  44.8 2.0 %slice.164 = f32[4,23,16,8,8]{1,4,3,2,0:T(8,128)} slice(f32[4,24,16,8,8]{1,4,3,2,0:T(8,128)S(1)} %copy-done.3), slice={[0:4], [1:24], [0:16], [0:8], [0:8]} | slice | bytes 753664 | tf_op jit(solution)/shard_map/jit(_roll_static)/slice | solution.py:74
  48.5 1.6 %gather_fusion = f32[128,768]{1,0:T(8,128)} fusion(f32[64,768]{1,0:T(8,128)S(1)} %reshape.421, s32[1024]{0:T(1024)S(1)} %get-tuple-element.54), kind=kCustom, calls=%fused_computation | custom fusion | bytes 786944 | tf_op jit(solution)/shard_map/jit(_take)/gather | solution.py:201
  50.0 2.0 %reshape.427 = f32[64,2,768]{2,1,0:T(2,128)} reshape(f32[128,768]{1,0:T(8,128)} %gather_fusion) | data formatting | bytes 786432 | tf_op jit(solution)/shard_map/jit(_take)/gather | solution.py:201
  52.1 2.0 %broadcast_select_fusion = f32[64,2,768]{2,1,0:T(2,128)} fusion(f32[64,2,768]{2,1,0:T(2,128)} %reshape.427, pred[64,2]{1,0:T(8,128)(4,1)S(1)} %copy.172), kind=kLoop, calls=%fused_computation.63 | loop fusion | flops 98304 | bytes 786560 | tf_op jit(solution)/shard_map/jit(_take)/select_n | solution.py:201
  54.1 10.5 %all-to-all-start.1 = ((f32[64,2,768]{2,1,0:T(2,128)}), f32[64,2,768]{2,1,0:T(2,128)}, u32[]{:S(2)}, u32[]{:S(2)}) async-start(f32[64,2,768]{2,1,0:T(2,128)} %broadcast_select_fusion), calls=%async_computation.1 | async-start | bytes 786432 | tf_op jit(solution)/shard_map/all_to_all | solution.py:204
  64.6 4.4 %slice_multiply_fusion.3 = (f32[4,24,16,7,8]{1,4,3,2,0:T(8,128)}, f32[4,24,16,7,8]{1,4,3,2,0:T(8,128)}) fusion(f32[4,24,16,8,8]{1,4,3,2,0:T(8,128)S(1)} %bitcast.157, f32[4,24,16,8,8]{1,4,3,2,0:T(8,128)} %copy-done.5), kind=kLoop, calls=%fused_computation.24 | loop fusion | flops 430080 | bytes 2064384 | tf_op jit(solution)/shard_map/mul | solution.py:65
  69.0 2.7 %slice_multiply_fusion.1 = (f32[4,24,16,8,7]{1,4,3,2,0:T(8,128)}, f32[4,24,16,8,7]{1,4,3,2,0:T(8,128)}) fusion(f32[4,24,16,8,8]{1,4,3,2,0:T(8,128)S(1)} %bitcast.158, f32[4,24,16,8,8]{1,4,3,2,0:T(8,128)S(1)} %copy-done.1), kind=kLoop, calls=%fused_computation.12 | loop fusion | flops 430080 | bytes 2064384 | tf_op jit(solution)/shard_map/mul | solution.py:63
  72.6 3.4 %gather.20 = f32[16,4,4,24,8]{4,3,2,1,0:T(8,128)} reshape(f32[64,768]{1,0:T(8,128)S(1)} %gather_fusion.2) | data formatting | bytes 393216 | tf_op jit(solution)/shard_map/jit(_take)/gather | solution.py:207
  75.9 3.2 %copy.177 = f32[16,4,4,24,8]{3,4,1,0,2:T(8,128)} copy(f32[16,4,4,24,8]{4,3,2,1,0:T(8,128)} %gather.20) | data formatting | bytes 393216 | tf_op jit(solution)/shard_map/jit(_take)/gather | solution.py:207
  80.4 1.5 %gather_fusion.1 = f32[64,768]{1,0:T(8,128)} fusion(f32[128,768]{1,0:T(8,128)S(1)} %reshape.422, s32[1024]{0:T(1024)} %pad_clamp_fusion.1), kind=kCustom, calls=%fused_computation.1 | custom fusion | bytes 393472 | tf_op jit(solution)/shard_map/jit(_take)/gather | solution.py:206
  81.8 3.8 %gather.18 = f32[16,4,4,24,8]{4,3,2,1,0:T(8,128)} reshape(f32[64,768]{1,0:T(8,128)} %gather_fusion.1) | data formatting | bytes 393216 | tf_op jit(solution)/shard_map/jit(_take)/gather | solution.py:206
  85.7 3.2 %copy.176 = f32[16,4,4,24,8]{3,4,1,0,2:T(8,128)} copy(f32[16,4,4,24,8]{4,3,2,1,0:T(8,128)} %gather.18) | data formatting | bytes 393216 | tf_op jit(solution)/shard_map/jit(_take)/gather | solution.py:206
  88.8 2.0 %select_bitcast_fusion = f32[4,24,16,4,8]{1,4,3,2,0:T(8,128)S(1)} fusion(f32[16,4,4,24,8]{3,4,1,0,2:T(8,128)} %copy.177, f32[16,4,4,24,8]{3,4,1,0,2:T(8,128)} %copy.176, pred[16,4]{1,0:T(8,128)(4,1)S(1)} %copy-done.22, pred[16,4]{1,0:T(8,128)(4,1)S(1)} %broadcast_in_dim.64, pred[16,4]{1,0:T(8,128)(4,1)S(1)} %broadcast_in_dim.62), kind=kLoop, calls=%fused_computation.41 | loop fusion | flops 147456 | bytes 590016 | tf_op jit(solution)/shard_map/transpose | solution.py:209
  93.1 7.5 %fusion.97 = (bf16[4,24,16,8,8]{1,4,3,2,0:T(8,128)(2,1)S(1)}, f32[4,24,16,8,8]{1,4,3,2,0:T(8,128)}) fusion(f32[4,24,16,1,8]{1,4,3,2,0:T(8,128)S(1)} %get-tuple-element.34, f32[4,24,16,1,8]{1,4,3,2,0:T(8,128)S(1)} %get-tuple-element.35, f32[4,24,16,8,8]{1,3,2,0,4:T(8,128)S(1)} %pad_add_fusion, f32[4,1,16,8,8]{1,4,3,2,0:T(8,128)S(1)} %bitcast.161, ...), kind=kLoop, calls=%fused_computation.192 | loop fusion | flops 2752512 | bytes 3780800 | tf_op jit(solution)/shard_map/convert_element_type | solution.py:215
  101.6 20.9 %all_to_all.30 = bf16[8,4,24,1,128]{4,2,3,1,0:T(8,128)(2,1)S(1)} all-to-all(bf16[8,4,24,1,128]{4,2,3,1,0:T(8,128)(2,1)S(1)} %constant_dynamic-update-slice_fusion), channel_id=1, replica_groups=mesh['blk'=64,'spec'=8] {'spec'}, dimensions={0} | all-to-all | bytes 393216 | tf_op jit(solution)/shard_map/all_to_all | solution.py:19
  126.7 3.5 %all-to-all-start.3 = ((f32[8,4,24,128]{3,1,2,0:T(4,128)}), f32[8,4,24,128]{3,1,2,0:T(4,128)S(1)}, u32[]{:S(2)}, u32[]{:S(2)}) async-start(f32[8,4,24,128]{3,1,2,0:T(4,128)} %copy.209), calls=%async_computation.3 | async-start | bytes 786432 | tf_op jit(solution)/shard_map/all_to_all | solution.py:223
  131.0 12.7 %all-to-all-done.3 = f32[8,4,24,128]{3,1,2,0:T(4,128)S(1)} async-done(((f32[8,4,24,128]{3,1,2,0:T(4,128)}), f32[8,4,24,128]{3,1,2,0:T(4,128)S(1)}, u32[]{:S(2)}, u32[]{:S(2)}) %all-to-all-start.3) | async-done | bytes 393248 | tf_op jit(solution)/shard_map/all_to_all | solution.py:223
  (149 shorter events, 30.8 us)
Async XLA Ops:
  5.0 41.8 %all-to-all-start = ((s32[64,1,2]{2,1,0:T(1,128)}), s32[64,1,2]{2,1,0:T(1,128)}, u32[]{:S(2)}, u32[]{:S(2)}) async-start(s32[64,1,2]{2,1,0:T(1,128)} %copy.170), calls=%async_computation | async-start | bytes 65536 | tf_op jit(solution)/shard_map/all_to_all | solution.py:202
  16.0 7.0 %copy-start.23 = (f32[4]{0:T(128)}, f32[4]{0:T(128)S(1)}, u32[]{:S(2)}) copy-start(f32[4]{0:T(128)S(1)} %get-tuple-element.49) | copy-start | bytes 52
  16.0 7.0 %copy-start.25 = (f32[4]{0:T(128)}, f32[4]{0:T(128)S(1)}, u32[]{:S(2)}) copy-start(f32[4]{0:T(128)S(1)} %broadcast_multiply_fusion.3) | copy-start | bytes 52
  19.5 3.6 %copy-start.11 = (f32[16,8,8]{2,1,0:T(8,128)}, f32[16,8,8]{2,1,0:T(8,128)S(1)}, u32[]{:S(2)}) copy-start(f32[16,8,8]{2,1,0:T(8,128)S(1)} %add.194) | copy-start | bytes 12292
  19.6 3.5 %copy-start.13 = (f32[16,8,8]{2,1,0:T(8,128)}, f32[16,8,8]{2,1,0:T(8,128)S(1)}, u32[]{:S(2)}) copy-start(f32[16,8,8]{2,1,0:T(8,128)S(1)} %add.197) | copy-start | bytes 12292
  20.4 2.7 %copy-start.15 = (f32[16,8,8]{2,1,0:T(8,128)}, f32[16,8,8]{2,1,0:T(8,128)S(1)}, u32[]{:S(2)}) copy-start(f32[16,8,8]{2,1,0:T(8,128)S(1)} %mul.536) | copy-start | bytes 12292
  23.1 2.6 %copy-start.5 = (f32[4,24,16,8,8]{1,4,3,2,0:T(8,128)}, f32[4,24,16,8,8]{1,4,3,2,0:T(8,128)S(1)}, u32[]{:S(2)}) copy-start(f32[4,24,16,8,8]{1,4,3,2,0:T(8,128)S(1)} %get-tuple-element.38) | copy-start | bytes 1179652
  36.8 3.5 %copy-start.27 = (pred[64]{0:T(512)(128)(4,1)S(1)}, pred[64]{0:T(512)(128)(4,1)}, u32[]{:S(2)}) copy-start(pred[64]{0:T(512)(128)(4,1)} %get-tuple-element.45) | copy-start | bytes 196
  36.8 3.6 %copy-start.29 = (pred[64]{0:T(512)(128)(4,1)S(1)}, pred[64]{0:T(512)(128)(4,1)}, u32[]{:S(2)}) copy-start(pred[64]{0:T(512)(128)(4,1)} %get-tuple-element.13) | copy-start | bytes 196
  41.1 3.7 %copy-start.3 = (f32[4,24,16,8,8]{1,4,3,2,0:T(8,128)S(1)}, f32[4,24,16,8,8]{1,4,3,2,0:T(8,128)}, u32[]{:S(2)}) copy-start(f32[4,24,16,8,8]{1,4,3,2,0:T(8,128)} %get-tuple-element.24) | copy-start | bytes 1179652
  44.8 3.1 %copy-start.30 = (s32[64]{0:T(128)S(1)}, s32[64]{0:T(128)}, u32[]{:S(2)}) copy-start(s32[64]{0:T(128)} %compare_select_fusion.2) | copy-start | bytes 772
  54.1 25.0 %all-to-all-start.1 = ((f32[64,2,768]{2,1,0:T(2,128)}), f32[64,2,768]{2,1,0:T(2,128)}, u32[]{:S(2)}, u32[]{:S(2)}) async-start(f32[64,2,768]{2,1,0:T(2,128)} %broadcast_select_fusion), calls=%async_computation.1 | async-start | bytes 786432 | tf_op jit(solution)/shard_map/all_to_all | solution.py:204
  64.6 4.5 %copy-start.1 = (f32[4,24,16,8,8]{1,4,3,2,0:T(8,128)S(1)}, f32[4,24,16,8,8]{1,4,3,2,0:T(8,128)}, u32[]{:S(2)}) copy-start(f32[4,24,16,8,8]{1,4,3,2,0:T(8,128)} %copy-done) | copy-start | bytes 1179652
  85.7 3.2 %copy-start.22 = (pred[16,4]{1,0:T(8,128)(4,1)S(1)}, pred[16,4]{1,0:T(8,128)(4,1)}, u32[]{:S(2)}) copy-start(pred[16,4]{1,0:T(8,128)(4,1)} %broadcast_in_dim.69) | copy-start | bytes 196
  100.6 22.0 %copy-start.18 = (bf16[2,32,32]{2,1,0:T(8,128)(2,1)S(1)}, bf16[2,32,32]{2,1,0:T(8,128)(2,1)}, u32[]{:S(2)}) copy-start(bf16[2,32,32]{2,1,0:T(8,128)(2,1)} %param.19) | copy-start | bytes 12292
  100.6 22.2 %copy-start.17 = (bf16[2,2,24,24]{3,2,1,0:T(8,128)(2,1)S(1)}, bf16[2,2,24,24]{3,2,1,0:T(8,128)(2,1)}, u32[]{:S(2)}) copy-start(bf16[2,2,24,24]{3,2,1,0:T(8,128)(2,1)} %param.20) | copy-start | bytes 13828
  101.5 22.3 %copy-start.28 = (f32[32]{0:T(128)S(1)}, f32[32]{0:T(128)}, u32[]{:S(2)}) copy-start(f32[32]{0:T(128)} %param.21) | copy-start | bytes 388
  125.1 5.0 %copy-start.19 = (s32[1024]{0:T(1024)S(1)}, s32[1024]{0:T(1024)}, u32[]{:S(2)}) copy-start(s32[1024]{0:T(1024)} %param.16) | copy-start | bytes 12292
  125.1 5.0 %copy-start.21 = (f32[2,1024]{1,0:T(2,128)S(1)}, f32[2,1024]{1,0:T(2,128)}, u32[]{:S(2)}) copy-start(f32[2,1024]{1,0:T(2,128)} %param.15) | copy-start | bytes 24580
  125.1 5.1 %copy-start.20 = (f32[1024]{0:T(1024)S(1)}, f32[1024]{0:T(1024)}, u32[]{:S(2)}) copy-start(f32[1024]{0:T(1024)} %param.12) | copy-start | bytes 12292
  125.2 5.1 %copy-start.24 = (f32[4]{0:T(128)S(1)}, f32[4]{0:T(128)}, u32[]{:S(2)}) copy-start(f32[4]{0:T(128)} %copy-done.23) | copy-start | bytes 52
  125.2 5.1 %copy-start.26 = (f32[4]{0:T(128)S(1)}, f32[4]{0:T(128)}, u32[]{:S(2)}) copy-start(f32[4]{0:T(128)} %copy-done.25) | copy-start | bytes 52
  125.2 5.2 %copy-start.6 = (f32[4,24,16,8,8]{1,4,3,2,0:T(8,128)S(1)}, f32[4,24,16,8,8]{1,4,3,2,0:T(8,128)}, u32[]{:S(2)}) copy-start(f32[4,24,16,8,8]{1,4,3,2,0:T(8,128)} %get-tuple-element.10) | copy-start | bytes 1179652
  126.7 17.0 %all-to-all-start.3 = ((f32[8,4,24,128]{3,1,2,0:T(4,128)}), f32[8,4,24,128]{3,1,2,0:T(4,128)S(1)}, u32[]{:S(2)}, u32[]{:S(2)}) async-start(f32[8,4,24,128]{3,1,2,0:T(4,128)} %copy.209), calls=%async_computation.3 | async-start | bytes 786432 | tf_op jit(solution)/shard_map/all_to_all | solution.py:223
  (10 other events, 21.6 us)
